TPU v7x, 128 devices: a whole 4x4x4 slice. The times are simulated.
128 devices in a mesh: req: 64 (over z, y, x), kv: 2 (over core).
Axes of the slice: x: 4, y: 4, z: 4, core: 2. Of those that a mesh axis runs over, the one named last changes fastest.
Arguments:
- queries: bfloat16 [16384, 2048], P(('req', 'kv')), may hold values from -6 to 6
- keys: bfloat16 [16384, 1024], P(('req', 'kv')), may hold values from -6 to 6
- values: bfloat16 [16384, 1024], P(('req', 'kv')), may hold values from -6 to 6
- residual: bfloat16 [16384, 3584], P(('req', 'kv'))
- segment_ids: int32 [16384], P(('req', 'kv')), may hold values from 127 to 16383, as said below
- regroup: int32 [16384], P(('req', 'kv')), may hold values from 0 to 16383, as said below
- out_weight: bfloat16 [2048, 3584], P('kv')
- attn_gain: float32 [3584], replicated, may hold values from 0.1 to 1.9
- pre_gain: float32 [3584], replicated, may hold values from 0.1 to 1.9
- gate_weight: bfloat16 [3584, 7168], P(None, 'kv'), may hold values from -0.09375 to 0.09375
- up_weight: bfloat16 [3584, 7168], P(None, 'kv'), may hold values from -0.09375 to 0.09375
- down_weight: bfloat16 [7168, 3584], P('kv')
- post_gain: float32 [3584], replicated, may hold values from 0.1 to 1.9
Outputs:
- layer_out: bfloat16 [16384, 3584], P(('req', 'kv'))
- key_cache_rows: bfloat16 [4, 16384, 256], P(None, ('req', 'kv'))
- value_cache_rows: bfloat16 [4, 16384, 256], P(None, ('req', 'kv'))
Inputs may be any that keep to these rules, and one draw needn't show every extreme that they name: `segment_ids`: A request is a run of consecutive slots carrying one id, the index of its last slot; no request runs from one index of req's 256 slots into the next. `regroup`: A permutation of the slots. Each device (in req+kv order) sends exactly one of its 128 slots to each of the 128 devices: for every pair of devices, exactly one slot of the first has its output row among the 128 rows of the second.
All inputs are finite; a program needn't handle non-finite values.
Results may differ from a plain program's by a relative error of at most 0.0095.
Values may be sent and summed in bfloat16 or wider, within the bound.
A program may use at most 192 MiB of HBM per device.

v0:
```python
import jax
import jax.numpy as jnp
from jax import lax
from jax.sharding import PartitionSpec as P

QUERY_HEADS = 8
KEY_VALUE_HEADS = 4
HEAD_ENTRIES = 256
WINDOW_REACH = 512
cap_value = 50.0
norm_eps = 1e-06


def from_behind(block, axis, distance):
    devices = range(lax.axis_size(axis))
    route = [(i - distance, i) for i in devices if i - distance in devices]
    return lax.ppermute(block, axis, route)


def rms_scale(values_in, gain_row):
    mean_square = jnp.mean(values_in * values_in, axis=-1, keepdims=True)
    return values_in * lax.rsqrt(mean_square + norm_eps) * gain_row


def key_mask(own_ids, key_ids, key_pos):
    distance = jnp.arange(own_ids.shape[0], dtype=jnp.int32)[:, None] - key_pos[None, :]
    return (own_ids[:, None] == key_ids[None, :]) & (distance >= 0) & (distance < WINDOW_REACH)


def block_terms(query_head_rows, key_heads, value_heads, allowed):
    raw_scores = jnp.einsum(
        "tkgd,skd->kgts", query_head_rows, key_heads, preferred_element_type=jnp.float32
    )
    scores = cap_value * jnp.tanh(raw_scores * HEAD_ENTRIES ** (-0.5) / cap_value)
    weights = jnp.where(allowed, jnp.exp(scores), 0.0)
    totals = jnp.sum(weights, axis=-1)
    numerator = jnp.einsum(
        "kgts,skd->tkgd",
        weights.astype(jnp.bfloat16),
        value_heads,
        preferred_element_type=jnp.float32,
    )
    return (numerator, totals)


def send_rows(normed_part, normed_pos, stream_part, key_portion, value_portion):
    received = (
        lax.all_to_all(normed_part, ("req", "kv"), split_axis=0, concat_axis=0, tiled=True),
        lax.all_to_all(normed_pos, ("req", "kv"), split_axis=0, concat_axis=0, tiled=True),
        lax.all_to_all(stream_part, ("req", "kv"), split_axis=0, concat_axis=0, tiled=True),
        lax.all_to_all(key_portion, ("req", "kv"), split_axis=0, concat_axis=0, tiled=True),
        lax.all_to_all(value_portion, ("req", "kv"), split_axis=0, concat_axis=0, tiled=True),
    )
    return received


def per_device(
    queries,
    keys,
    values,
    residual,
    segment_ids,
    regroup,
    out_weight,
    attn_gain,
    pre_gain,
    gate_weight,
    up_weight,
    down_weight,
    post_gain,
):
    resident_rows = queries.shape[0]
    grouped_heads = QUERY_HEADS // KEY_VALUE_HEADS
    query_head_rows = queries.reshape(resident_rows, KEY_VALUE_HEADS, grouped_heads, HEAD_ENTRIES)
    own_ids = segment_ids + 1
    base_pos = jnp.arange(resident_rows, dtype=jnp.int32)
    key_collections = [(keys, values, own_ids, base_pos)]
    moved_keys, moved_values, moved_ids = from_behind((keys, values, own_ids), "kv", 1)
    key_collections.append((moved_keys, moved_values, moved_ids, base_pos - resident_rows))
    gathered_keys = jnp.concatenate(
        [key_collection[0] for key_collection in key_collections], axis=0
    ).reshape(-1, KEY_VALUE_HEADS, HEAD_ENTRIES)
    gathered_values = jnp.concatenate(
        [key_collection[1] for key_collection in key_collections], axis=0
    ).reshape(-1, KEY_VALUE_HEADS, HEAD_ENTRIES)
    all_ids = jnp.concatenate([key_collection[2] for key_collection in key_collections], axis=0)
    all_pos = jnp.concatenate([key_collection[3] for key_collection in key_collections], axis=0)
    numerator, totals = block_terms(
        query_head_rows, gathered_keys, gathered_values, key_mask(own_ids, all_ids, all_pos)
    )
    attended_output = (
        (numerator / jnp.transpose(totals, (2, 0, 1))[..., None])
        .astype(jnp.bfloat16)
        .reshape(resident_rows, QUERY_HEADS * HEAD_ENTRIES)
    )
    head_rows = lax.all_to_all(attended_output, "kv", split_axis=1, concat_axis=0, tiled=True)
    picked = head_rows
    projected = lax.psum_scatter(
        jnp.dot(picked, out_weight, preferred_element_type=jnp.float32).astype(jnp.bfloat16),
        "kv",
        scatter_dimension=0,
        tiled=True,
    ).astype(jnp.float32)
    stream = (residual.astype(jnp.float32) + rms_scale(projected, attn_gain)).astype(jnp.bfloat16)
    normed = rms_scale(stream.astype(jnp.float32), pre_gain).astype(jnp.bfloat16)
    row_order = jnp.argsort(regroup)
    destination_rows = regroup[row_order]
    sorted_normed = normed[row_order]
    sorted_stream = stream[row_order]
    sorted_keys = keys[row_order]
    sorted_values = values[row_order]
    received = send_rows(
        sorted_normed, destination_rows % resident_rows, sorted_stream, sorted_keys, sorted_values
    )
    placed = jnp.argsort(received[1])
    own_normed = received[0][placed]
    group_normed = lax.all_gather(own_normed, "kv", axis=0, tiled=True)
    own_stream = received[2][placed]
    resident_keys = received[3][placed]
    resident_values = received[4][placed]
    picked = group_normed
    gate_part = jnp.dot(picked, gate_weight, preferred_element_type=jnp.float32)
    up_part = jnp.dot(picked, up_weight, preferred_element_type=jnp.float32)
    active = (jax.nn.gelu(gate_part, approximate=True) * up_part).astype(jnp.bfloat16)
    ffw_sum = lax.psum_scatter(
        jnp.dot(active, down_weight, preferred_element_type=jnp.float32).astype(jnp.bfloat16),
        "kv",
        scatter_dimension=0,
        tiled=True,
    ).astype(jnp.float32)
    layer_out = (own_stream.astype(jnp.float32) + rms_scale(ffw_sum, post_gain)).astype(
        jnp.bfloat16
    )
    key_cache_rows = resident_keys.reshape(resident_rows, KEY_VALUE_HEADS, HEAD_ENTRIES).transpose(
        1, 0, 2
    )
    value_cache_rows = resident_values.reshape(
        resident_rows, KEY_VALUE_HEADS, HEAD_ENTRIES
    ).transpose(1, 0, 2)
    return (layer_out, key_cache_rows, value_cache_rows)


def solution(mesh):
    placed = (
        P(("req", "kv"), None),
        P(("req", "kv"), None),
        P(("req", "kv"), None),
        P(("req", "kv"), None),
        P(("req", "kv")),
        P(("req", "kv")),
        P("kv", None),
        P(),
        P(),
        P(None, "kv"),
        P(None, "kv"),
        P("kv", None),
        P(),
    )
    return jax.shard_map(
        per_device,
        mesh=mesh,
        in_specs=placed,
        out_specs=(
            P(("req", "kv"), None),
            P(None, ("req", "kv"), None),
            P(None, ("req", "kv"), None),
        ),
        check_vma=False,
    )
```

profile of v0, /device:TPU:1, one launch (start us, length us, event | category | flops | bytes accessed | tf_op | source)
XLA Modules:
  0.0 216.2 jit_solution(5172984267959892114)
XLA Ops:
  17.9 4.2 %all_to_all.76 = bf16[128,2,1024]{2,0,1:T(8,128)(2,1)S(1)} all-to-all(bf16[128,2,1024]{2,0,1:T(8,128)(2,1)S(1)} %copy.50), channel_id=1, replica_groups=mesh['req'=64,'kv'=2] {'kv'}, dimensions={1} | all-to-all | bytes 1048576 | tf_op jit(solution)/shard_map/all_to_all | solution.py:96
  22.1 6.4 %convolution_convert_fusion.1 = bf16[256,3584]{1,0:T(8,128)(2,1)} fusion(bf16[256,1024]{1,0:T(8,128)(2,1)S(1)} %bitcast.76, bf16[1024,3584]{1,0:T(8,128)(2,1)} %param.19), kind=kOutput, calls=%fused_computation.13 | convolution fusion | flops 1879965696 | bytes 9699328 | tf_op jit(solution)/shard_map/dot_general | solution.py:99
  29.2 2.5 %sort.31 = (s32[128]{0:T(128)}, s32[128]{0:T(128)S(1)}) sort(s32[128]{0:T(128)S(1)} %copy-done, s32[128]{0:T(128)S(1)} %iota.18), dimensions={0}, to_apply=%region_3.4 | sort | flops 896 | bytes 2048 | tf_op jit(solution)/shard_map/jit(argsort)/sort | solution.py:106
  33.8 10.9 %all-to-all-start.2 = ((s32[128,1,1]{2,1,0:T(1,128)}), s32[128,1,1]{2,1,0:T(1,128)S(1)}, u32[]{:S(2)}, u32[]{:S(2)}) async-start(s32[128,1,1]{2,1,0:T(1,128)} %copy.52), calls=%async_computation.3 | async-start | bytes 131072 | tf_op jit(solution)/shard_map/all_to_all | solution.py:49
  46.2 1.8 fusion.12
  52.2 2.0 all-to-all-done.2
  54.2 7.8 %all-to-all-start.3 = ((bf16[128,2,1792]{2,1,0:T(2,128)(2,1)}), bf16[128,2,1792]{2,1,0:T(2,128)(2,1)S(1)}, u32[]{:S(2)}, u32[]{:S(2)}) async-start(bf16[128,2,1792]{2,1,0:T(2,128)(2,1)} %reshape.194), calls=%async_computation.4 | async-start | bytes 1835008 | tf_op jit(solution)/shard_map/all_to_all | solution.py:48
  62.0 2.4 %reduce = s32[128]{0:T(128)S(1)} reduce(s32[128,1,1]{2,1,0:T(1,128)S(1)} %all-to-all-done.2, s32[]{:T(128)} %constant.17.clone.1), dimensions={1,2}, to_apply=%all_to_all.59.reduce_sub_computation | reduce | bytes 1028 | tf_op jit(solution)/shard_map/all_to_all | solution.py:49
  64.4 2.5 %sort.32 = (s32[128]{0:T(128)}, s32[128]{0:T(128)S(1)}) sort(s32[128]{0:T(128)S(1)} %reduce, s32[128]{0:T(128)S(1)} %iota.19), dimensions={0}, to_apply=%region_4.5 | sort | flops 896 | bytes 2048 | tf_op jit(solution)/shard_map/jit(argsort)/sort | solution.py:115
  67.0 13.0 %all-to-all-done.3 = bf16[128,2,1792]{2,1,0:T(2,128)(2,1)S(1)} async-done(((bf16[128,2,1792]{2,1,0:T(2,128)(2,1)}), bf16[128,2,1792]{2,1,0:T(2,128)(2,1)S(1)}, u32[]{:S(2)}, u32[]{:S(2)}) %all-to-all-start.3) | async-done | bytes 917536 | tf_op jit(solution)/shard_map/all_to_all | solution.py:48
  79.9 2.1 reshape.195
  82.0 1.6 copy.79
  83.7 2.0 gather_fusion.4
  86.0 9.3 %all-gather.3.cloned.1.call-done = bf16[256,3584]{1,0:T(8,128)(2,1)} async-done(((bf16[128,3584]{1,0:T(8,128)(2,1)}), bf16[256,3584]{1,0:T(8,128)(2,1)}) %all-gather.3.cloned.1.call-update) | async-done | bytes 1835024 | tf_op jit(solution)/shard_map/all_gather | solution.py:117
  95.3 17.1 %fusion.43 = f32[256,3584]{1,0:T(8,128)} fusion(bf16[256,3584]{1,0:T(8,128)(2,1)} %all-gather.3.cloned.1.call-done, bf16[3584,3584]{1,0:T(8,128)(2,1)} %param.22), kind=kOutput, calls=%fused_computation.86 | convolution fusion | flops 6576668672 | bytes 31195136 | tf_op jit(solution)/shard_map/dot_general | solution.py:122
  112.4 24.6 %convolution_convert_fusion = bf16[256,3584]{1,0:T(8,128)(2,1)} fusion(bf16[3584,3584]{1,0:T(8,128)(2,1)} %param.24, bf16[256,3584]{1,0:T(8,128)(2,1)S(1)} %copy-done.7, bf16[3584,3584]{1,0:T(8,128)(2,1)} %param.23, f32[256,3584]{1,0:T(8,128)} %fusion.43), kind=kOutput, calls=%fused_computation.12 | convolution fusion | flops 13163429888 | bytes 58720256 | tf_op jit(solution)/shard_map/dot_general | solution.py:126
  140.3 9.2 %all-to-all-start.4 = ((bf16[128,2,512]{2,1,0:T(2,128)(2,1)}), bf16[128,2,512]{2,1,0:T(2,128)(2,1)S(1)}, u32[]{:S(2)}, u32[]{:S(2)}) async-start(bf16[128,2,512]{2,1,0:T(2,128)(2,1)} %reshape.198), calls=%async_computation.6 | async-start | bytes 524288 | tf_op jit(solution)/shard_map/all_to_all | solution.py:51
  152.0 8.7 %all-to-all-done.4 = bf16[128,2,512]{2,1,0:T(2,128)(2,1)S(1)} async-done(((bf16[128,2,512]{2,1,0:T(2,128)(2,1)}), bf16[128,2,512]{2,1,0:T(2,128)(2,1)S(1)}, u32[]{:S(2)}, u32[]{:S(2)}) %all-to-all-start.4) | async-done | bytes 262176 | tf_op jit(solution)/shard_map/all_to_all | solution.py:51
  160.6 4.4 %all-to-all-start.5 = ((bf16[128,2,512]{2,1,0:T(2,128)(2,1)}), bf16[128,2,512]{2,1,0:T(2,128)(2,1)S(1)}, u32[]{:S(2)}, u32[]{:S(2)}) async-start(bf16[128,2,512]{2,1,0:T(2,128)(2,1)} %reshape.200), calls=%async_computation.7 | async-start | bytes 524288 | tf_op jit(solution)/shard_map/all_to_all | solution.py:52
  168.5 7.6 %all-to-all-done.5 = bf16[128,2,512]{2,1,0:T(2,128)(2,1)S(1)} async-done(((bf16[128,2,512]{2,1,0:T(2,128)(2,1)}), bf16[128,2,512]{2,1,0:T(2,128)(2,1)S(1)}, u32[]{:S(2)}, u32[]{:S(2)}) %all-to-all-start.5) | async-done | bytes 262176 | tf_op jit(solution)/shard_map/all_to_all | solution.py:52
  176.1 5.1 %all-to-all-start.1 = ((bf16[128,2,1792]{2,1,0:T(2,128)(2,1)}), bf16[128,2,1792]{2,1,0:T(2,128)(2,1)}, u32[]{:S(2)}, u32[]{:S(2)}) async-start(bf16[128,2,1792]{2,1,0:T(2,128)(2,1)} %reshape.196), calls=%async_computation.2 | async-start | bytes 1835008 | tf_op jit(solution)/shard_map/all_to_all | solution.py:50
  184.5 14.5 %all-to-all-done.1 = bf16[128,2,1792]{2,1,0:T(2,128)(2,1)} async-done(((bf16[128,2,1792]{2,1,0:T(2,128)(2,1)}), bf16[128,2,1792]{2,1,0:T(2,128)(2,1)}, u32[]{:S(2)}, u32[]{:S(2)}) %all-to-all-start.1) | async-done | bytes 917536 | tf_op jit(solution)/shard_map/all_to_all | solution.py:50
  199.0 5.4 %reshape.197 = bf16[128,1,3584]{2,1,0:T(2,128)(2,1)S(1)} reshape(bf16[128,2,1792]{2,1,0:T(2,128)(2,1)} %all-to-all-done.1) | data formatting | bytes 1835008
  207.2 2.5 %fusion.18 = bf16[128,3584]{1,0:T(8,128)(2,1)} fusion(bf16[128,3584]{1,0:T(8,128)(2,1)} %reduce-scatter.5.cloned.1.call-done, bf16[128,3584]{1,0:T(8,128)(2,1)S(1)} %gather_fusion.2, f32[3584]{0:T(1024)S(1)} %copy-done.6, f32[128]{0:T(128)S(1)} %add_rsqrt_fusion), kind=kLoop, calls=%fused_computation.37 | loop fusion | flops 2752512 | bytes 2767360 | tf_op jit(solution)/shard_map/convert_element_type | solution.py:131
  (81 shorter events, 34.4 us)
Async XLA Ops:
  7.2 37.5 %reduce-scatter.3.cloned.1.call-start = ((), (), s32[]{:S(2)}) async-start(), calls=%async_computation.8 | async-start | bytes 2752512 | tf_op jit(solution)/shard_map/reduce_scatter | solution.py:98
  7.9 6.5 %collective-permute-start.1 = (s32[128]{0:T(128)S(1)}, s32[128]{0:T(128)S(1)}, u32[]{:S(2)}, u32[]{:S(2)}) collective-permute-start(s32[128]{0:T(128)S(1)} %broadcast_add_fusion), channel_id=1, source_target_pairs={{0,1},{2,3},{4,5},{6,7},{8,9},{10,11},{12,13},{14,15},{16,17},{18,... | collective-permute-start | bytes 1544 | tf_op jit(solution)/shard_map/ppermute | solution.py:17
  10.3 6.4 %collective-permute-start.2 = (bf16[128,1024]{0,1:T(8,128)(2,1)S(1)}, bf16[128,1024]{0,1:T(8,128)(2,1)S(1)}, u32[]{:S(2)}, u32[]{:S(2)}) collective-permute-start(bf16[128,1024]{0,1:T(8,128)(2,1)S(1)} %copy.46), channel_id=1, source_target_pairs={{0,1},{2,3},{4,5},{6,7},{8,9},{10,11},{12,13},{14,15},{16,17},{18,... | collective-permute-start | bytes 786440 | tf_op jit(solution)/shard_map/ppermute | solution.py:17
  11.6 4.0 %collective-permute-start = (bf16[128,1024]{1,0:T(8,128)(2,1)}, bf16[128,1024]{1,0:T(8,128)(2,1)S(1)}, u32[]{:S(2)}, u32[]{:S(2)}) collective-permute-start(bf16[128,1024]{1,0:T(8,128)(2,1)} %param.15), channel_id=1, source_target_pairs={{0,1},{2,3},{4,5},{6,7},{8,9},{10,11},{12,13},{14,15},{16,17},{18,... | collective-permute-start | bytes 786440 | tf_op jit(solution)/shard_map/ppermute | solution.py:17
  28.6 0.7 copy-start
  28.6 17.6 %copy-start.3 = (bf16[128,3584]{1,0:T(8,128)(2,1)S(1)}, bf16[128,3584]{1,0:T(8,128)(2,1)}, u32[]{:S(2)}) copy-start(bf16[128,3584]{1,0:T(8,128)(2,1)} %param.16) | copy-start | bytes 2752516
  28.6 17.6 %copy-start.4 = (f32[3584]{0:T(1024)S(1)}, f32[3584]{0:T(1024)}, u32[]{:S(2)}) copy-start(f32[3584]{0:T(1024)} %param.20) | copy-start | bytes 43012
  33.8 20.4 %all-to-all-start.2 = ((s32[128,1,1]{2,1,0:T(1,128)}), s32[128,1,1]{2,1,0:T(1,128)S(1)}, u32[]{:S(2)}, u32[]{:S(2)}) async-start(s32[128,1,1]{2,1,0:T(1,128)} %copy.52), calls=%async_computation.3 | async-start | bytes 131072 | tf_op jit(solution)/shard_map/all_to_all | solution.py:49
  44.7 3.3 %copy-start.5 = (f32[3584]{0:T(1024)S(1)}, f32[3584]{0:T(1024)}, u32[]{:S(2)}) copy-start(f32[3584]{0:T(1024)} %param.21) | copy-start | bytes 43012
  54.2 25.8 %all-to-all-start.3 = ((bf16[128,2,1792]{2,1,0:T(2,128)(2,1)}), bf16[128,2,1792]{2,1,0:T(2,128)(2,1)S(1)}, u32[]{:S(2)}, u32[]{:S(2)}) async-start(bf16[128,2,1792]{2,1,0:T(2,128)(2,1)} %reshape.194), calls=%async_computation.4 | async-start | bytes 1835008 | tf_op jit(solution)/shard_map/all_to_all | solution.py:48
  62.0 33.3 %all-gather.3.cloned.1.call-start = ((), (), s32[]{:S(2)}) async-start(), calls=%async_computation.10 | async-start | bytes 2752512 | tf_op jit(solution)/shard_map/all_gather | solution.py:117
  85.7 120.0 %reduce-scatter.5.cloned.1.call-start = ((), (), s32[]{:S(2)}) async-start(), calls=%async_computation.9 | async-start | bytes 2752512 | tf_op jit(solution)/shard_map/reduce_scatter | solution.py:125
  95.3 17.1 %copy-start.7 = (bf16[256,3584]{1,0:T(8,128)(2,1)S(1)}, bf16[256,3584]{1,0:T(8,128)(2,1)}, u32[]{:S(2)}) copy-start(bf16[256,3584]{1,0:T(8,128)(2,1)} %all-gather.3.cloned.1.call-done) | copy-start | bytes 5505028
  136.9 0.9 copy-start.1
  137.9 11.6 %copy-start.2 = (bf16[128,1024]{1,0:T(8,128)(2,1)S(1)}, bf16[128,1024]{1,0:T(8,128)(2,1)}, u32[]{:S(2)}) copy-start(bf16[128,1024]{1,0:T(8,128)(2,1)} %param.15) | copy-start | bytes 786436
  140.3 20.3 %all-to-all-start.4 = ((bf16[128,2,512]{2,1,0:T(2,128)(2,1)}), bf16[128,2,512]{2,1,0:T(2,128)(2,1)S(1)}, u32[]{:S(2)}, u32[]{:S(2)}) async-start(bf16[128,2,512]{2,1,0:T(2,128)(2,1)} %reshape.198), calls=%async_computation.6 | async-start | bytes 524288 | tf_op jit(solution)/shard_map/all_to_all | solution.py:51
  160.6 15.5 %all-to-all-start.5 = ((bf16[128,2,512]{2,1,0:T(2,128)(2,1)}), bf16[128,2,512]{2,1,0:T(2,128)(2,1)S(1)}, u32[]{:S(2)}, u32[]{:S(2)}) async-start(bf16[128,2,512]{2,1,0:T(2,128)(2,1)} %reshape.200), calls=%async_computation.7 | async-start | bytes 524288 | tf_op jit(solution)/shard_map/all_to_all | solution.py:52
  176.1 22.9 %all-to-all-start.1 = ((bf16[128,2,1792]{2,1,0:T(2,128)(2,1)}), bf16[128,2,1792]{2,1,0:T(2,128)(2,1)}, u32[]{:S(2)}, u32[]{:S(2)}) async-start(bf16[128,2,1792]{2,1,0:T(2,128)(2,1)} %reshape.196), calls=%async_computation.2 | async-start | bytes 1835008 | tf_op jit(solution)/shard_map/all_to_all | solution.py:50
  204.6 2.6 %copy-start.6 = (f32[3584]{0:T(1024)S(1)}, f32[3584]{0:T(1024)}, u32[]{:S(2)}) copy-start(f32[3584]{0:T(1024)} %param.25) | copy-start | bytes 43012
Sparse Core Ops, SparseCore 0:
  28.7 15.0 reduce-scatter.2
  85.9 9.4 all-gather.2
  137.1 13.3 reduce-scatter.4
where the time goes:
time: 217 us; the launch traced here: 216 us
  waiting for transfers between devices  56.2 us (26%)
  matrix products  48.9 us (23%)
  starting transfers between devices  41.6 us (19%)
  local copies, waits for them, and re-layouts  30.5 us (14%)
  other arithmetic  20.6 us (9%)
  between operations  14.1 us (6%)
  blocking collectives  4.22 us (2%)
    dot_general x1, matrix products, per_device(): jnp.dot(active, down_weight, preferred_element_type=jnp.float32)  24.6 us
    dot_general x1, matrix products, per_device(): gate_part = jnp.dot(picked, gate_weight, preferred_element_type=jnp.float32)  17.1 us
    unnamed x29, local copies, waits for them, and re-layouts  16.6 us
    all_to_all x1, waiting for transfers between devices, send_rows(): lax.all_to_all(stream_part, ('req', 'kv'), split_axis=0, concat_axis=0, t...  14.5 us
    all_to_all x1, waiting for transfers between devices, send_rows(): lax.all_to_all(normed_part, ('req', 'kv'), split_axis=0, concat_axis=0, t...  13 us
    all_to_all x1, starting transfers between devices, send_rows(): lax.all_to_all(normed_pos, ('req', 'kv'), split_axis=0, concat_axis=0, ti...  10.9 us
    all_gather x1, waiting for transfers between devices, per_device(): group_normed = lax.all_gather(own_normed, 'kv', axis=0, tiled=True)  9.35 us
    all_to_all x1, starting transfers between devices, send_rows(): lax.all_to_all(key_portion, ('req', 'kv'), split_axis=0, concat_axis=0, t...  9.19 us
  transfers between devices with their start and end apart: 11, of which 7 were waited for; matrix products, arithmetic and copies ran while one was open for 18% of the time, Pallas kernels for 0%

commit v1 on v0

--- a/solution.py
+++ b/solution.py
@@ -114,7 +114,14 @@
     )
     placed = jnp.argsort(received[1])
     own_normed = received[0][placed]
-    group_normed = lax.all_gather(own_normed, "kv", axis=0, tiled=True)
+
+    def begin_pipes_on(state):
+        pile = []
+        for _ in range(lax.axis_size("kv")):
+            pile.append(state)
+        return jnp.concatenate(lax.all_to_all(jnp.stack(pile), "kv", 0, 0), 0)
+
+    group_normed = begin_pipes_on(own_normed)
     own_stream = received[2][placed]
     resident_keys = received[3][placed]
     resident_values = received[4][placed]

time: 217 us -> 204 us (0.940)
  waiting for transfers between devices: 56.2 us -> 46.9 us
  blocking collectives: 4.22 us -> 9.99 us
  starting transfers between devices: 41.6 us -> 36 us
  matrix products: 48.9 us -> 45.5 us
    all_gather x1 -> x0, waiting for transfers between devices: 9.35 us -> none  [per_device(): group_normed = lax.all_gather(own_normed, 'kv', axis=0, tiled=True)]
    all_to_all x0 -> x1, blocking collectives: none -> 5.77 us  [begin_pipes_on(): return jnp.concatenate(lax.all_to_all(jnp.stack(pile), 'kv', 0, 0), 0)]
    all_to_all x1, starting transfers between devices: 9.19 us -> 3.82 us  [send_rows(): lax.all_to_all(key_portion, ('req', 'kv'), split_axis=0, concat_axis=0, t...]
    dot_general x1, matrix products: 17.1 us -> 13.7 us  [per_device(): gate_part = jnp.dot(picked, gate_weight, preferred_element_type=jnp.float32)]
    unnamed x29 -> x27, local copies, waits for them, and re-layouts: 16.6 us -> 16.6 us
  transfers between devices with their start and end apart: 11 -> 10, of which waited for: 7 -> 6; matrix products, arithmetic and copies ran while one was open for 18% -> 19% of each run, Pallas kernels for 0% -> 0%
where the time goes in v1:
time: 204 us; the launch traced here: 203 us
  waiting for transfers between devices  46.9 us (23%)
  matrix products  45.5 us (22%)
  starting transfers between devices  36 us (18%)
  local copies, waits for them, and re-layouts  29.6 us (15%)
  other arithmetic  20.8 us (10%)
  between operations  14.4 us (7%)
  blocking collectives  9.99 us (5%)
    dot_general x1, matrix products, per_device(): jnp.dot(active, down_weight, preferred_element_type=jnp.float32)  24.6 us
    unnamed x27, local copies, waits for them, and re-layouts  16.6 us
    all_to_all x1, waiting for transfers between devices, send_rows(): lax.all_to_all(stream_part, ('req', 'kv'), split_axis=0, concat_axis=0, t...  14.5 us
    dot_general x1, matrix products, per_device(): gate_part = jnp.dot(picked, gate_weight, preferred_element_type=jnp.float32)  13.7 us
    all_to_all x1, waiting for transfers between devices, send_rows(): lax.all_to_all(normed_part, ('req', 'kv'), split_axis=0, concat_axis=0, t...  13 us
    all_to_all x1, starting transfers between devices, send_rows(): lax.all_to_all(normed_pos, ('req', 'kv'), split_axis=0, concat_axis=0, ti...  10.9 us
    all_to_all x1, waiting for transfers between devices, send_rows(): lax.all_to_all(key_portion, ('req', 'kv'), split_axis=0, concat_axis=0, t...  8.71 us
    all_to_all x1, starting transfers between devices, send_rows(): lax.all_to_all(normed_part, ('req', 'kv'), split_axis=0, concat_axis=0, t...  7.8 us
  transfers between devices with their start and end apart: 10, of which 6 were waited for; matrix products, arithmetic and copies ran while one was open for 19% of the time, Pallas kernels for 0%

profile of v1, /device:TPU:1, one launch (start us, length us, event | category | flops | bytes accessed | tf_op | source)
XLA Modules:
  0.0 203.2 jit_solution(318032628038433108)
XLA Ops:
  17.9 4.2 %all_to_all.81 = bf16[128,2,1024]{2,0,1:T(8,128)(2,1)S(1)} all-to-all(bf16[128,2,1024]{2,0,1:T(8,128)(2,1)S(1)} %copy.50), channel_id=1, replica_groups=mesh['req'=64,'kv'=2] {'kv'}, dimensions={1} | all-to-all | bytes 1048576 | tf_op jit(solution)/shard_map/all_to_all | solution.py:96
  22.1 6.4 %convolution_convert_fusion.1 = bf16[256,3584]{1,0:T(8,128)(2,1)} fusion(bf16[256,1024]{1,0:T(8,128)(2,1)S(1)} %bitcast.81, bf16[1024,3584]{1,0:T(8,128)(2,1)} %param.19), kind=kOutput, calls=%fused_computation.13 | convolution fusion | flops 1879965696 | bytes 9699328 | tf_op jit(solution)/shard_map/dot_general | solution.py:99
  29.2 2.5 %sort.31 = (s32[128]{0:T(128)}, s32[128]{0:T(128)S(1)}) sort(s32[128]{0:T(128)S(1)} %copy-done, s32[128]{0:T(128)S(1)} %iota.18), dimensions={0}, to_apply=%region_3.4 | sort | flops 896 | bytes 2048 | tf_op jit(solution)/shard_map/jit(argsort)/sort | solution.py:106
  33.8 10.9 %all-to-all-start.2 = ((s32[128,1,1]{2,1,0:T(1,128)}), s32[128,1,1]{2,1,0:T(1,128)S(1)}, u32[]{:S(2)}, u32[]{:S(2)}) async-start(s32[128,1,1]{2,1,0:T(1,128)} %copy.52), calls=%async_computation.3 | async-start | bytes 131072 | tf_op jit(solution)/shard_map/all_to_all | solution.py:49
  44.7 1.4 fusion.8
  46.2 1.8 fusion.12
  52.2 2.0 all-to-all-done.2
  54.2 7.8 %all-to-all-start.3 = ((bf16[128,2,1792]{2,1,0:T(2,128)(2,1)}), bf16[128,2,1792]{2,1,0:T(2,128)(2,1)S(1)}, u32[]{:S(2)}, u32[]{:S(2)}) async-start(bf16[128,2,1792]{2,1,0:T(2,128)(2,1)} %reshape.197), calls=%async_computation.4 | async-start | bytes 1835008 | tf_op jit(solution)/shard_map/all_to_all | solution.py:48
  62.0 2.4 %reduce = s32[128]{0:T(128)S(1)} reduce(s32[128,1,1]{2,1,0:T(1,128)S(1)} %all-to-all-done.2, s32[]{:T(128)} %constant.17.clone.1), dimensions={1,2}, to_apply=%all_to_all.62.reduce_sub_computation | reduce | bytes 1028 | tf_op jit(solution)/shard_map/all_to_all | solution.py:49
  64.4 2.5 %sort.32 = (s32[128]{0:T(128)}, s32[128]{0:T(128)S(1)}) sort(s32[128]{0:T(128)S(1)} %reduce, s32[128]{0:T(128)S(1)} %iota.19), dimensions={0}, to_apply=%region_4.5 | sort | flops 896 | bytes 2048 | tf_op jit(solution)/shard_map/jit(argsort)/sort | solution.py:115
  67.0 13.0 %all-to-all-done.3 = bf16[128,2,1792]{2,1,0:T(2,128)(2,1)S(1)} async-done(((bf16[128,2,1792]{2,1,0:T(2,128)(2,1)}), bf16[128,2,1792]{2,1,0:T(2,128)(2,1)S(1)}, u32[]{:S(2)}, u32[]{:S(2)}) %all-to-all-start.3) | async-done | bytes 917536 | tf_op jit(solution)/shard_map/all_to_all | solution.py:48
  79.9 2.1 %reshape.198 = bf16[128,1,3584]{2,1,0:T(2,128)(2,1)} reshape(bf16[128,2,1792]{2,1,0:T(2,128)(2,1)S(1)} %all-to-all-done.3) | data formatting | bytes 1835008
  82.0 1.6 copy.79
  85.0 5.8 %all_to_all.82 = bf16[2,128,3584]{2,1,0:T(8,128)(2,1)S(1)} all-to-all(bf16[2,128,3584]{2,1,0:T(8,128)(2,1)S(1)} %pad_maximum_fusion), channel_id=1, replica_groups=mesh['req'=64,'kv'=2] {'kv'}, dimensions={0} | all-to-all | bytes 3670016 | tf_op jit(solution)/shard_map/all_to_all | solution.py:122
  90.7 13.7 %fusion.43 = f32[256,3584]{1,0:T(8,128)} fusion(bf16[256,3584]{1,0:T(8,128)(2,1)S(1)} %bitcast.72, bf16[3584,3584]{1,0:T(8,128)(2,1)} %param.22), kind=kOutput, calls=%fused_computation.87 | convolution fusion | flops 6576668672 | bytes 31195136 | tf_op jit(solution)/shard_map/dot_general | solution.py:129
  104.4 24.6 %convolution_convert_fusion = bf16[256,3584]{1,0:T(8,128)(2,1)} fusion(bf16[3584,3584]{1,0:T(8,128)(2,1)} %param.24, bf16[256,3584]{1,0:T(8,128)(2,1)S(1)} %bitcast.73, bf16[3584,3584]{1,0:T(8,128)(2,1)} %param.23, f32[256,3584]{1,0:T(8,128)} %fusion.43), kind=kOutput, calls=%fused_computation.12 | convolution fusion | flops 13163429888 | bytes 58720256 | tf_op jit(solution)/shard_map/dot_general | solution.py:133
  132.3 3.8 %all-to-all-start.5 = ((bf16[128,2,512]{2,1,0:T(2,128)(2,1)}), bf16[128,2,512]{2,1,0:T(2,128)(2,1)S(1)}, u32[]{:S(2)}, u32[]{:S(2)}) async-start(bf16[128,2,512]{2,1,0:T(2,128)(2,1)} %reshape.201), calls=%async_computation.7 | async-start | bytes 524288 | tf_op jit(solution)/shard_map/all_to_all | solution.py:51
  138.6 8.7 %all-to-all-done.5 = bf16[128,2,512]{2,1,0:T(2,128)(2,1)S(1)} async-done(((bf16[128,2,512]{2,1,0:T(2,128)(2,1)}), bf16[128,2,512]{2,1,0:T(2,128)(2,1)S(1)}, u32[]{:S(2)}, u32[]{:S(2)}) %all-to-all-start.5) | async-done | bytes 262176 | tf_op jit(solution)/shard_map/all_to_all | solution.py:51
  147.3 4.4 %all-to-all-start.6 = ((bf16[128,2,512]{2,1,0:T(2,128)(2,1)}), bf16[128,2,512]{2,1,0:T(2,128)(2,1)S(1)}, u32[]{:S(2)}, u32[]{:S(2)}) async-start(bf16[128,2,512]{2,1,0:T(2,128)(2,1)} %reshape.203), calls=%async_computation.8 | async-start | bytes 524288 | tf_op jit(solution)/shard_map/all_to_all | solution.py:52
  155.2 7.6 %all-to-all-done.6 = bf16[128,2,512]{2,1,0:T(2,128)(2,1)S(1)} async-done(((bf16[128,2,512]{2,1,0:T(2,128)(2,1)}), bf16[128,2,512]{2,1,0:T(2,128)(2,1)S(1)}, u32[]{:S(2)}, u32[]{:S(2)}) %all-to-all-start.6) | async-done | bytes 262176 | tf_op jit(solution)/shard_map/all_to_all | solution.py:52
  162.8 5.1 %all-to-all-start.1 = ((bf16[128,2,1792]{2,1,0:T(2,128)(2,1)}), bf16[128,2,1792]{2,1,0:T(2,128)(2,1)}, u32[]{:S(2)}, u32[]{:S(2)}) async-start(bf16[128,2,1792]{2,1,0:T(2,128)(2,1)} %reshape.199), calls=%async_computation.2 | async-start | bytes 1835008 | tf_op jit(solution)/shard_map/all_to_all | solution.py:50
  171.2 14.5 %all-to-all-done.1 = bf16[128,2,1792]{2,1,0:T(2,128)(2,1)} async-done(((bf16[128,2,1792]{2,1,0:T(2,128)(2,1)}), bf16[128,2,1792]{2,1,0:T(2,128)(2,1)}, u32[]{:S(2)}, u32[]{:S(2)}) %all-to-all-start.1) | async-done | bytes 917536 | tf_op jit(solution)/shard_map/all_to_all | solution.py:50
  185.7 5.4 %reshape.200 = bf16[128,1,3584]{2,1,0:T(2,128)(2,1)S(1)} reshape(bf16[128,2,1792]{2,1,0:T(2,128)(2,1)} %all-to-all-done.1) | data formatting | bytes 1835008
  193.9 2.5 %fusion.18 = bf16[128,3584]{1,0:T(8,128)(2,1)} fusion(bf16[128,3584]{1,0:T(8,128)(2,1)} %reduce-scatter.5.cloned.1.call-done, bf16[128,3584]{1,0:T(8,128)(2,1)S(1)} %gather_fusion.2, f32[3584]{0:T(1024)S(1)} %copy-done.6, f32[128]{0:T(128)S(1)} %add_rsqrt_fusion), kind=kLoop, calls=%fused_computation.37 | loop fusion | flops 2752512 | bytes 2767360 | tf_op jit(solution)/shard_map/convert_element_type | solution.py:138
  (78 shorter events, 34.0 us)
Async XLA Ops:
  7.2 37.5 %reduce-scatter.3.cloned.1.call-start = ((), (), s32[]{:S(2)}) async-start(), calls=%async_computation.9 | async-start | bytes 2752512 | tf_op jit(solution)/shard_map/reduce_scatter | solution.py:98
  7.9 6.5 %collective-permute-start.1 = (s32[128]{0:T(128)S(1)}, s32[128]{0:T(128)S(1)}, u32[]{:S(2)}, u32[]{:S(2)}) collective-permute-start(s32[128]{0:T(128)S(1)} %broadcast_add_fusion), channel_id=1, source_target_pairs={{0,1},{2,3},{4,5},{6,7},{8,9},{10,11},{12,13},{14,15},{16,17},{18,... | collective-permute-start | bytes 1544 | tf_op jit(solution)/shard_map/ppermute | solution.py:17
  10.3 6.4 %collective-permute-start.2 = (bf16[128,1024]{0,1:T(8,128)(2,1)S(1)}, bf16[128,1024]{0,1:T(8,128)(2,1)S(1)}, u32[]{:S(2)}, u32[]{:S(2)}) collective-permute-start(bf16[128,1024]{0,1:T(8,128)(2,1)S(1)} %copy.46), channel_id=1, source_target_pairs={{0,1},{2,3},{4,5},{6,7},{8,9},{10,11},{12,13},{14,15},{16,17},{18,... | collective-permute-start | bytes 786440 | tf_op jit(solution)/shard_map/ppermute | solution.py:17
  11.6 4.0 %collective-permute-start = (bf16[128,1024]{1,0:T(8,128)(2,1)}, bf16[128,1024]{1,0:T(8,128)(2,1)S(1)}, u32[]{:S(2)}, u32[]{:S(2)}) collective-permute-start(bf16[128,1024]{1,0:T(8,128)(2,1)} %param.15), channel_id=1, source_target_pairs={{0,1},{2,3},{4,5},{6,7},{8,9},{10,11},{12,13},{14,15},{16,17},{18,... | collective-permute-start | bytes 786440 | tf_op jit(solution)/shard_map/ppermute | solution.py:17
  28.6 0.7 copy-start
  28.6 17.6 %copy-start.3 = (bf16[128,3584]{1,0:T(8,128)(2,1)S(1)}, bf16[128,3584]{1,0:T(8,128)(2,1)}, u32[]{:S(2)}) copy-start(bf16[128,3584]{1,0:T(8,128)(2,1)} %param.16) | copy-start | bytes 2752516
  28.6 17.6 %copy-start.4 = (f32[3584]{0:T(1024)S(1)}, f32[3584]{0:T(1024)}, u32[]{:S(2)}) copy-start(f32[3584]{0:T(1024)} %param.20) | copy-start | bytes 43012
  33.8 20.4 %all-to-all-start.2 = ((s32[128,1,1]{2,1,0:T(1,128)}), s32[128,1,1]{2,1,0:T(1,128)S(1)}, u32[]{:S(2)}, u32[]{:S(2)}) async-start(s32[128,1,1]{2,1,0:T(1,128)} %copy.52), calls=%async_computation.3 | async-start | bytes 131072 | tf_op jit(solution)/shard_map/all_to_all | solution.py:49
  44.7 3.3 %copy-start.5 = (f32[3584]{0:T(1024)S(1)}, f32[3584]{0:T(1024)}, u32[]{:S(2)}) copy-start(f32[3584]{0:T(1024)} %param.21) | copy-start | bytes 43012
  54.2 25.8 %all-to-all-start.3 = ((bf16[128,2,1792]{2,1,0:T(2,128)(2,1)}), bf16[128,2,1792]{2,1,0:T(2,128)(2,1)S(1)}, u32[]{:S(2)}, u32[]{:S(2)}) async-start(bf16[128,2,1792]{2,1,0:T(2,128)(2,1)} %reshape.197), calls=%async_computation.4 | async-start | bytes 1835008 | tf_op jit(solution)/shard_map/all_to_all | solution.py:48
  62.0 130.4 %reduce-scatter.5.cloned.1.call-start = ((), (), s32[]{:S(2)}) async-start(), calls=%async_computation.10 | async-start | bytes 2752512 | tf_op jit(solution)/shard_map/reduce_scatter | solution.py:132
  129.0 0.9 copy-start.1
  129.9 6.3 %copy-start.2 = (bf16[128,1024]{1,0:T(8,128)(2,1)S(1)}, bf16[128,1024]{1,0:T(8,128)(2,1)}, u32[]{:S(2)}) copy-start(bf16[128,1024]{1,0:T(8,128)(2,1)} %param.15) | copy-start | bytes 786436
  132.3 15.0 %all-to-all-start.5 = ((bf16[128,2,512]{2,1,0:T(2,128)(2,1)}), bf16[128,2,512]{2,1,0:T(2,128)(2,1)S(1)}, u32[]{:S(2)}, u32[]{:S(2)}) async-start(bf16[128,2,512]{2,1,0:T(2,128)(2,1)} %reshape.201), calls=%async_computation.7 | async-start | bytes 524288 | tf_op jit(solution)/shard_map/all_to_all | solution.py:51
  147.3 15.5 %all-to-all-start.6 = ((bf16[128,2,512]{2,1,0:T(2,128)(2,1)}), bf16[128,2,512]{2,1,0:T(2,128)(2,1)S(1)}, u32[]{:S(2)}, u32[]{:S(2)}) async-start(bf16[128,2,512]{2,1,0:T(2,128)(2,1)} %reshape.203), calls=%async_computation.8 | async-start | bytes 524288 | tf_op jit(solution)/shard_map/all_to_all | solution.py:52
  162.8 22.9 %all-to-all-start.1 = ((bf16[128,2,1792]{2,1,0:T(2,128)(2,1)}), bf16[128,2,1792]{2,1,0:T(2,128)(2,1)}, u32[]{:S(2)}, u32[]{:S(2)}) async-start(bf16[128,2,1792]{2,1,0:T(2,128)(2,1)} %reshape.199), calls=%async_computation.2 | async-start | bytes 1835008 | tf_op jit(solution)/shard_map/all_to_all | solution.py:50
  191.3 2.6 %copy-start.6 = (f32[3584]{0:T(1024)S(1)}, f32[3584]{0:T(1024)}, u32[]{:S(2)}) copy-start(f32[3584]{0:T(1024)} %param.25) | copy-start | bytes 43012
Sparse Core Ops, SparseCore 0:
  28.7 15.0 reduce-scatter.2
  129.1 7.9 reduce-scatter.4
